TPU v7x, 128 devices: a whole 4x4x4 slice. The times are simulated.
128 devices in a mesh: section: 2 (over core), seq: 4 (over x), dp: 16 (over z, y).
Axes of the slice: x: 4, y: 4, z: 4, core: 2. Of those that a mesh axis runs over, the one named last changes fastest.
Arguments:
- section_input: bfloat16 [2, 16, 512, 4096], P('section', 'dp', 'seq'), may hold values from -6 to 6
- saved_qkv: bfloat16 [2, 16, 512, 3, 2048], P('section', 'dp', None, None, 'seq'), may hold values from -14 to 14
- modulation: float32 [2, 16, 2, 4096], P('section', 'dp'), may hold values from -4 to 4
- w_qkv: bfloat16 [2, 4096, 3, 2048], P('section', 'dp', None, 'seq'), may hold values from -0.09375 to 0.09375
- w_out: bfloat16 [2, 2048, 4096], P('section', 'seq'), may hold values from -0.125 to 0.125
- lengths: int32 [16], P('dp'), may hold values from 1 to 512, 5120 in all
- student_out: bfloat16 [16, 512, 4096], P('dp', 'seq'), may hold values from -6 to 6
- teacher_target: bfloat16 [16, 512, 4096], P('dp', 'seq'), may hold values from -6 to 6
Outputs:
- grad_input: bfloat16 [2, 16, 512, 4096], P('section', 'dp', 'seq')
- grad_out: bfloat16 [2, 2048, 4096], P('section', 'seq', 'dp')
Inputs may be any that keep to these rules, and one draw needn't show every extreme that they name: `lengths`: at least one micro-batch is 512 tokens long.
All inputs are finite; a program needn't handle non-finite values. No bound on the sum of `lengths` on one device may be relied on, other than what follows from the above.
Results may differ from a plain program's by a relative error of at most 0.014.
Values may be sent and summed in bfloat16 or wider, within the bound.
A program may use at most 192 MiB of HBM per device.

v0:
```python
import math
import jax
import jax.numpy as jnp
from jax import lax
from jax.sharding import PartitionSpec as P

HEAD_DIM = 128


def in_blocks(value, dim, count):
    dims = value.shape
    tiles = value.reshape(*dims[:dim], count, dims[dim] // count, *dims[dim + 1 :])
    return jnp.moveaxis(tiles, dim, 0)


def sum_at_owner(value, axis, dim):
    count = lax.axis_size(axis)
    tiles = lax.all_to_all(in_blocks(value, dim, count), axis, 0, 0, tiled=True)
    return jnp.sum(tiles, axis=0)


def shifted(value, axis, steps):
    count = lax.axis_size(axis)
    initial, last = (max(0, -steps), min(count, count - steps))
    return lax.ppermute(value, axis, [(source, source + steps) for source in range(initial, last)])


def widen(tensor):
    return lax.optimization_barrier(tensor).astype(jnp.float32)


def contract_rows(left_side, right_side):
    return lax.dot_general(
        left_side, right_side, (((0,), (0,)), ((), ())), preferred_element_type=jnp.float32
    )


def layer_norm_parts(tokens):
    values = tokens.astype(jnp.float32)
    center = values - jnp.mean(values, axis=-1, keepdims=True)
    variance = jnp.mean(center * center, axis=-1, keepdims=True)
    inverse = lax.rsqrt(variance + 1e-06)
    return (center * inverse, inverse)


def attend_backward(saved_rows, d_attn, live_keys, head_size):
    row_total = saved_rows.shape[0]
    feature_width = saved_rows.shape[2]
    head_count = feature_width // head_size
    queries = saved_rows[:, 0].reshape(row_total, head_count, head_size).astype(jnp.float32)
    key_rows = saved_rows[:, 1].reshape(row_total, head_count, head_size).astype(jnp.float32)
    value_rows = saved_rows[:, 2].reshape(row_total, head_count, head_size).astype(jnp.float32)
    factor = 1.0 / math.sqrt(head_size)
    scores = jnp.einsum("qhd,khd->hqk", queries, key_rows) * factor
    scores = jnp.where(live_keys[None, None, :], scores, -1e30)
    peak_score = jnp.max(scores, axis=-1, keepdims=True)
    weights = jnp.exp(scores - peak_score)
    weights = weights / jnp.sum(weights, axis=-1, keepdims=True)
    rounded = widen(weights.astype(jnp.bfloat16))
    attn_mixed = jnp.einsum("hqk,khd->qhd", rounded, value_rows).astype(jnp.bfloat16)
    upstream = d_attn.reshape(row_total, head_count, head_size).astype(jnp.float32)
    d_weights = jnp.einsum("qhd,khd->hqk", upstream, value_rows)
    delta_rows = jnp.einsum("qhd,qhd->hq", upstream, widen(attn_mixed))
    d_scores = widen((weights * (d_weights - delta_rows[:, :, None]) * factor).astype(jnp.bfloat16))
    grad_q = jnp.einsum("hqk,khd->qhd", d_scores, key_rows).astype(jnp.bfloat16)
    grad_k = jnp.einsum("hqk,qhd->khd", d_scores, queries).astype(jnp.bfloat16)
    grad_v = jnp.einsum("hqk,qhd->khd", rounded, upstream).astype(jnp.bfloat16)
    stacked = jnp.stack([grad_q, grad_k, grad_v], axis=1).reshape(row_total, 3, feature_width)
    return (attn_mixed.reshape(row_total, feature_width), stacked)


def body(section_input, saved_qkv, modulation, w_qkv, w_out, lengths, student_out, teacher_target):
    section_total = lax.axis_size("section")
    section_pos = lax.axis_index("section")
    seq_pos = lax.axis_index("seq")
    micro_count = section_input.shape[1]
    shard_rows = section_input.shape[2]
    model_width = section_input.shape[3]
    capacity = saved_qkv.shape[2]
    local_width = saved_qkv.shape[4]
    inputs = section_input[0]
    saved_all = saved_qkv[0]
    mods = modulation[0]
    weight_rows = lax.all_gather(w_qkv[0], "dp", axis=0, tiled=True)
    weight_flat = weight_rows.reshape(model_width, 3 * local_width)
    weight_out = w_out[0]
    normed_all, inverse_all = layer_norm_parts(inputs)
    positions = seq_pos * shard_rows + jnp.arange(shard_rows, dtype=jnp.int32)
    row_live = positions[None, :] < lengths[:, None]
    gap = student_out.astype(jnp.float32) - teacher_target.astype(jnp.float32)
    loss_grad = jnp.where(row_live[:, :, None], gap, 0.0).astype(jnp.bfloat16)
    key_positions = jnp.arange(capacity, dtype=jnp.int32)

    def attend_live(saved_rows, d_attn, live_keys):
        attn_mixed, d_saved = attend_backward(saved_rows, d_attn, live_keys, HEAD_DIM)
        return (attn_mixed, d_saved.reshape(capacity, 3 * local_width))

    def section_work(d_output, slot_index, is_live):
        mod_rows = lax.dynamic_index_in_dim(mods, slot_index, 0, False)
        scale_term = mod_rows[0]
        gate_term = mod_rows[1]
        d_branch = (gate_term * d_output.astype(jnp.float32)).astype(jnp.bfloat16)
        d_branch = jnp.where(is_live, d_branch, jnp.zeros_like(d_branch))
        branch_full = lax.all_gather(d_branch, "seq", axis=0, tiled=True)
        live_length = lengths[slot_index]
        live_keys = key_positions < live_length
        saved_rows = lax.dynamic_index_in_dim(saved_all, slot_index, 0, False)

        def attend_branch(branch_rows):
            d_attn = jnp.dot(branch_rows, weight_out.T, preferred_element_type=jnp.float32).astype(
                jnp.bfloat16
            )
            return attend_live(saved_rows, d_attn, live_keys)

        def attend_none(branch_rows):
            return (
                jnp.zeros((capacity, local_width), jnp.bfloat16),
                jnp.zeros((capacity, 3 * local_width), jnp.bfloat16),
            )

        attn_mixed, flat_grads = lax.cond(is_live, attend_branch, attend_none, branch_full)
        d_mod = sum_at_owner(
            lax.cond(
                is_live,
                lambda start_row: jnp.dot(
                    flat_grads, weight_flat.T, preferred_element_type=jnp.float32
                ),
                lambda start_row: jnp.zeros(
                    (shard_rows * lax.axis_size("seq"), model_width), jnp.float32
                ),
                jnp.int32(0),
            ),
            "seq",
            0,
        )
        normed = lax.dynamic_index_in_dim(normed_all, slot_index, 0, False)
        inverse = lax.dynamic_index_in_dim(inverse_all, slot_index, 0, False)
        d_norm = d_mod * (1.0 + scale_term)
        d_layer = inverse * (
            d_norm
            - jnp.mean(d_norm, axis=-1, keepdims=True)
            - normed * jnp.mean(d_norm * normed, axis=-1, keepdims=True)
        )
        d_input = (d_output.astype(jnp.float32) + d_layer).astype(jnp.bfloat16)
        d_input = jnp.where(is_live, d_input, jnp.zeros_like(d_input))
        return (d_input, attn_mixed, branch_full)

    def put_slot(store, fresh, slot_index, is_live):
        older = lax.dynamic_index_in_dim(store, slot_index, 0, False)
        return lax.dynamic_update_index_in_dim(
            store, jnp.where(is_live, fresh, older), slot_index, 0
        )

    def tick(tick_num, carry):
        incoming, grads_in, mixed_store, branch_store = carry
        slot_raw = tick_num - (section_total - 1 - section_pos)
        is_live = jnp.logical_and(slot_raw >= 0, slot_raw < micro_count)
        slot_index = jnp.clip(slot_raw, 0, micro_count - 1)
        last_grad = lax.dynamic_index_in_dim(loss_grad, slot_index, 0, False)
        d_output = jnp.where(section_pos == section_total - 1, last_grad, incoming)
        d_input, attn_mixed, branch_full = section_work(d_output, slot_index, is_live)
        grads_in = put_slot(grads_in, d_input, slot_index, is_live)
        mixed_store = put_slot(mixed_store, attn_mixed, slot_index, is_live)
        branch_store = put_slot(branch_store, branch_full, slot_index, is_live)
        incoming = shifted(d_input, "section", -1)
        return (incoming, grads_in, mixed_store, branch_store)

    start_carry = (
        jnp.zeros((shard_rows, model_width), jnp.bfloat16),
        jnp.zeros((micro_count, shard_rows, model_width), jnp.bfloat16),
        jnp.zeros((micro_count, capacity, local_width), jnp.bfloat16),
        jnp.zeros((micro_count, capacity, model_width), jnp.bfloat16),
    )
    final_carry = lax.fori_loop(0, section_total + micro_count - 1, tick, start_carry)
    grads_in = final_carry[1]
    mixed_store = final_carry[2]
    branch_store = final_carry[3]
    out_local = contract_rows(
        mixed_store.reshape(micro_count * capacity, local_width),
        branch_store.reshape(micro_count * capacity, model_width),
    )
    out_slice = lax.psum_scatter(out_local, "dp", scatter_dimension=1, tiled=True)
    grad_input = grads_in[None]
    grad_out = out_slice.astype(jnp.bfloat16)[None]
    return (grad_input, grad_out)


def solution(mesh):
    in_specs = (
        P("section", "dp", "seq", None),
        P("section", "dp", None, None, "seq"),
        P("section", "dp", None, None),
        P("section", "dp", None, "seq"),
        P("section", "seq", None),
        P("dp"),
        P("dp", "seq", None),
        P("dp", "seq", None),
    )
    out_specs = (P("section", "dp", "seq", None), P("section", "seq", "dp"))
    return jax.shard_map(body, mesh=mesh, in_specs=in_specs, out_specs=out_specs, check_vma=False)
```

profile of v0, /device:TPU:0, one launch (start us, length us, event | category | flops | bytes accessed | tf_op | source)
XLA Modules:
  0.0 575.2 jit_solution(12609359654335451927)
XLA Ops:
  7.2 2.3 copy.33
  10.3 2.7 copy.32
  13.6 3.3 fusion.29
  17.0 96.1 %all-gather.4.cloned.1.call-done = bf16[1,4096,3,512]{1,3,2,0:T(8,128)(2,1)} async-done(((bf16[1,256,3,512]{1,3,2,0:T(8,128)(2,1)}), bf16[1,4096,3,512]{1,3,2,0:T(8,128)(2,1)}) %all-gather.4.cloned.1.call-update) | async-done | bytes 12582928 | tf_op jit(solution)/shard_map/all_gather | solution.py:84
  113.0 16.6 %copy.34 = bf16[4096,1536]{1,0:T(8,128)(2,1)} copy(bf16[4096,1536]{0,1:T(8,128)(2,1)} %bitcast.151) | data formatting | bytes 25165824
  129.7 0.8 broadcast_in_dim.88
  130.5 1.1 broadcast_in_dim.87
  131.7 2.6 broadcast_in_dim.89
  134.2 339.5 %while.22 = (s32[]{:T(128)}, bf16[128,4096]{1,0:T(8,128)(2,1)S(1)}, bf16[1,128,4096]{2,1,0:T(8,128)(2,1)}, bf16[1,512,512]{1,2,0:T(8,128)(2,1)}, bf16[1,512,4096...) while((s32[]{:T(128)}, bf16[128,4096]{1,0:T(8,128)(2,1)S(1)}, ...), condition=%wide.region_12.13_spmd.clone, body=%wide.region_2.12_spmd.clone.sunk | while | flops 10230434816 | bytes 286427392 | solution.py:174
  134.3 1.4 fusion.60
  135.8 48.5 %all-gather.6.cloned.1.call-done = bf16[512,4096]{1,0:T(8,128)(2,1)} async-done(((bf16[128,4096]{1,0:T(8,128)(2,1)}), bf16[512,4096]{1,0:T(8,128)(2,1)}) %all-gather.6.cloned.1.call-update) | async-done | bytes 4194320 | tf_op jit(solution)/shard_map/while/body/eval_jaxpr/all_gather | solution.py:104
  184.2 1.3 conditional.6
  184.3 1.3 broadcast.151
  185.6 4.3 conditional.7
  185.6 4.3 broadcast.153
  189.9 5.8 %all-to-all-start = ((f32[4,128,4096]{2,1,0:T(8,128)}), f32[4,128,4096]{2,1,0:T(8,128)}, u32[]{:S(2)}, u32[]{:S(2)}) async-start(f32[4,128,4096]{2,1,0:T(8,128)} %bitcast.137), calls=%async_computation | async-start | bytes 16777216 | tf_op jit(solution)/shard_map/while/body/eval_jaxpr/all_to_all | solution.py:18
  196.6 71.3 %all-to-all-done = f32[4,128,4096]{2,1,0:T(8,128)} async-done(((f32[4,128,4096]{2,1,0:T(8,128)}), f32[4,128,4096]{2,1,0:T(8,128)}, u32[]{:S(2)}, u32[]{:S(2)}) %all-to-all-start) | async-done | bytes 8388640 | tf_op jit(solution)/shard_map/while/body/eval_jaxpr/all_to_all | solution.py:18
  267.9 4.2 reduce_sum.85
  272.2 2.1 multiply_reduce_fusion.2
  274.6 2.5 fusion.61
  277.1 1.4 collective-permute-start
  278.8 1.1 fusion.63
  279.9 22.3 %collective-permute-done = bf16[128,4096]{1,0:T(8,128)(2,1)S(1)} collective-permute-done((bf16[128,4096]{1,0:T(8,128)(2,1)S(1)}, bf16[128,4096]{1,0:T(8,128)(2,1)S(1)}, u32[]{:S(2)}, u32[]{:S(2)}) %collective-permute-start) | collective-permute-done | bytes 1048608 | tf_op jit(solution)/shard_map/while/body/eval_jaxpr/ppermute | solution.py:25
  302.3 1.4 fusion.60
  303.7 50.5 %all-gather.6.cloned.1.call-done = bf16[512,4096]{1,0:T(8,128)(2,1)} async-done(((bf16[128,4096]{1,0:T(8,128)(2,1)}), bf16[512,4096]{1,0:T(8,128)(2,1)}) %all-gather.6.cloned.1.call-update) | async-done | bytes 4194320 | tf_op jit(solution)/shard_map/while/body/eval_jaxpr/all_gather | solution.py:104
  354.2 17.4 %conditional.6 = (bf16[512,512]{0,1:T(8,128)(2,1)S(1)}, bf16[512,1536]{0,1:T(8,128)(2,1)}) conditional(s32[]{:T(128)} %convert_element_type.172, () %tuple.86, (s32[1]{0:T(128)}, s32[512]{0:T(512)S(1)}, bf16[1,512,3,512]{1,3,2,0:T(8,128)(2,1)}, bf16[512,4096]{1,0:T(8,128)(2,1)}, bf16[512,4096]{1,0:T(8,128)(2,1)}) %tuple.87), branch_computations={%region_3.3_spmd, %region_4.6_spmd} | conditional | flops 3773561856 | bytes 101756056 | solution.py:121
  354.9 1.5 fusion.35
  356.3 3.6 fusion.36
  360.0 2.9 fusion.7
  363.4 1.5 copy-done.16
  364.9 2.4 fusion.11
  367.3 0.9 multiply_convert_fusion
  368.2 0.8 fusion.9
  369.0 0.8 fusion.8
  370.3 1.4 pad_maximum_fusion
  371.6 12.2 %conditional.7 = (f32[512,4096]{1,0:T(8,128)}) conditional(s32[]{:T(128)} %convert_element_type.172, () %tuple.85, (bf16[512,1536]{0,1:T(8,128)(2,1)}, bf16[4096,1536]{1,0:T(8,128)(2,1)}) %tuple.88), branch_computations={%region_7.7_spmd, %region_8.8_spmd} | conditional | flops 6442450944 | bytes 22544392 | solution.py:123
  371.6 12.2 %fusion.37 = f32[512,4096]{1,0:T(8,128)} fusion(bf16[512,1536]{0,1:T(8,128)(2,1)} %get-tuple-element.422, bf16[4096,1536]{1,0:T(8,128)(2,1)} %get-tuple-element.358), kind=kOutput, calls=%fused_computation.65 | convolution fusion | flops 6442450944 | bytes 22544384 | tf_op jit(solution)/shard_map/while/body/eval_jaxpr/cond/branch_1_fun/dot_general | solution.py:125
  383.8 5.8 %all-to-all-start = ((f32[4,128,4096]{2,1,0:T(8,128)}), f32[4,128,4096]{2,1,0:T(8,128)}, u32[]{:S(2)}, u32[]{:S(2)}) async-start(f32[4,128,4096]{2,1,0:T(8,128)} %bitcast.137), calls=%async_computation | async-start | bytes 16777216 | tf_op jit(solution)/shard_map/while/body/eval_jaxpr/all_to_all | solution.py:18
  390.6 69.1 %all-to-all-done = f32[4,128,4096]{2,1,0:T(8,128)} async-done(((f32[4,128,4096]{2,1,0:T(8,128)}), f32[4,128,4096]{2,1,0:T(8,128)}, u32[]{:S(2)}, u32[]{:S(2)}) %all-to-all-start) | async-done | bytes 8388640 | tf_op jit(solution)/shard_map/while/body/eval_jaxpr/all_to_all | solution.py:18
  459.7 4.2 reduce_sum.85
  463.9 2.1 multiply_reduce_fusion.2
  466.4 2.5 fusion.61
  468.9 1.4 collective-permute-start
  470.6 1.1 fusion.63
  471.7 1.9 collective-permute-done
  473.7 7.9 %fusion.26 = f32[512,4096]{1,0:T(8,128)} fusion(bf16[1,512,4096]{2,1,0:T(8,128)(2,1)} %get-tuple-element.385, bf16[1,512,512]{1,2,0:T(8,128)(2,1)} %get-tuple-element.384), kind=kOutput, calls=%fused_computation.48 | convolution fusion | flops 2147483648 | bytes 13107200 | tf_op jit(solution)/shard_map/dot_general | solution.py:33
  481.7 85.2 %reduce-scatter.2.cloned.1.call-done = f32[512,256]{1,0:T(8,128)} async-done(((f32[512,4096]{1,0:T(8,128)}), f32[512,256]{1,0:T(8,128)}) %reduce-scatter.2.cloned.1.call-update) | async-done | bytes 524304 | tf_op jit(solution)/shard_map/reduce_scatter | solution.py:182
  566.9 1.8 convert_bitcast_fusion.1
  (77 shorter events, 5.7 us)
Async XLA Ops:
  7.2 105.9 %all-gather.4.cloned.1.call-start = ((), (), s32[]{:S(2)}) async-start(), calls=%async_computation.3 | async-start | bytes 13369344 | tf_op jit(solution)/shard_map/all_gather | solution.py:84
  9.5 3.5 copy-start.13
  10.3 3.4 copy-start.14
  131.7 2.6 copy-start.15
  134.2 1.5 copy-start.3
  134.2 50.0 %all-gather.6.cloned.1.call-start = ((), (), s32[]{:S(2)}) async-start(), calls=%async_computation.4 | async-start | bytes 5242880 | tf_op jit(solution)/shard_map/while/body/eval_jaxpr/all_gather | solution.py:104
  189.9 5.8 %copy-start.11 = (bf16[1,512,512]{1,2,0:T(8,128)(2,1)S(1)}, bf16[1,512,512]{1,2,0:T(8,128)(2,1)}, u32[]{:S(2)}) copy-start(bf16[1,512,512]{1,2,0:T(8,128)(2,1)} %get-tuple-element.624) | copy-start | bytes 1572868 | tf_op jit(solution)/shard_map/while
  189.9 78.1 %all-to-all-start = ((f32[4,128,4096]{2,1,0:T(8,128)}), f32[4,128,4096]{2,1,0:T(8,128)}, u32[]{:S(2)}, u32[]{:S(2)}) async-start(f32[4,128,4096]{2,1,0:T(8,128)} %bitcast.137), calls=%async_computation | async-start | bytes 16777216 | tf_op jit(solution)/shard_map/while/body/eval_jaxpr/all_to_all | solution.py:18
  195.8 0.8 copy-start.12
  272.1 2.2 copy-start
  272.1 2.5 copy-start.9
  274.6 4.0 copy-start.1
  274.6 4.2 copy-start.4
  277.1 2.7 copy-start.10
  277.1 25.1 %collective-permute-start = (bf16[128,4096]{1,0:T(8,128)(2,1)S(1)}, bf16[128,4096]{1,0:T(8,128)(2,1)S(1)}, u32[]{:S(2)}, u32[]{:S(2)}) collective-permute-start(bf16[128,4096]{1,0:T(8,128)(2,1)S(1)} %get-tuple-element.596), channel_id=1, source_target_pairs={{64,0},{65,1},{66,2},{67,3},{68,4},{69,5},{70,6},{71,7},{72,8},{73... | collective-permute-start | bytes 3145736 | tf_op jit(solution)/shard_map/while/body/eval_jaxpr/ppermute | solution.py:25
  279.9 22.3 %copy-start.2 = (bf16[1,512,4096]{2,1,0:T(8,128)(2,1)}, bf16[1,512,4096]{2,1,0:T(8,128)(2,1)S(1)}, u32[]{:S(2)}) copy-start(bf16[1,512,4096]{2,1,0:T(8,128)(2,1)S(1)} %fusion.63) | copy-start | bytes 12582916 | tf_op jit(solution)/shard_map/while
  302.2 1.5 copy-start.3
  302.2 52.0 %all-gather.6.cloned.1.call-start = ((), (), s32[]{:S(2)}) async-start(), calls=%async_computation.4 | async-start | bytes 5242880 | tf_op jit(solution)/shard_map/while/body/eval_jaxpr/all_gather | solution.py:104
  360.0 3.4 copy-start.5
  360.0 4.9 copy-start.16
  363.4 3.9 copy-start.7
  364.9 2.4 copy-start.6
  370.3 1.4 copy-start.8
  383.8 5.8 %copy-start.11 = (bf16[1,512,512]{1,2,0:T(8,128)(2,1)S(1)}, bf16[1,512,512]{1,2,0:T(8,128)(2,1)}, u32[]{:S(2)}) copy-start(bf16[1,512,512]{1,2,0:T(8,128)(2,1)} %get-tuple-element.624) | copy-start | bytes 1572868 | tf_op jit(solution)/shard_map/while
  383.8 75.9 %all-to-all-start = ((f32[4,128,4096]{2,1,0:T(8,128)}), f32[4,128,4096]{2,1,0:T(8,128)}, u32[]{:S(2)}, u32[]{:S(2)}) async-start(f32[4,128,4096]{2,1,0:T(8,128)} %bitcast.137), calls=%async_computation | async-start | bytes 16777216 | tf_op jit(solution)/shard_map/while/body/eval_jaxpr/all_to_all | solution.py:18
  389.8 0.8 copy-start.12
  463.9 2.2 copy-start
  463.9 2.5 copy-start.9
  466.4 4.0 copy-start.1
  466.4 4.2 copy-start.4
  468.9 2.7 copy-start.10
  468.9 4.7 collective-permute-start
  471.7 2.1 copy-start.2
  473.7 93.2 %reduce-scatter.2.cloned.1.call-start = ((), (), s32[]{:S(2)}) async-start(), calls=%async_computation.2 | async-start | bytes 8912896 | tf_op jit(solution)/shard_map/reduce_scatter | solution.py:182
Sparse Core Ops, SparseCore 0:
  10.7 102.2 all-gather.3
  136.7 47.4 all-gather.5
  304.7 49.4 all-gather.5
  481.8 85.0 reduce-scatter.1
where the time goes:
time: 576 us; the launch traced here: 575 us
  waiting for transfers between devices  445 us (77%)
  local copies, waits for them, and re-layouts  37.6 us (7%)
  other arithmetic  33.7 us (6%)
  matrix products  29.5 us (5%)
  starting transfers between devices  14.5 us (3%)
  between operations  14.5 us (3%)
    all_to_all x2, waiting for transfers between devices, sum_at_owner(): tiles = lax.all_to_all(in_blocks(value, dim, count), axis, 0, 0, tiled=True)  140 us
    all_gather x2, waiting for transfers between devices, section_work(): branch_full = lax.all_gather(d_branch, 'seq', axis=0, tiled=True)  99 us
    all_gather x1, waiting for transfers between devices, body(): weight_rows = lax.all_gather(w_qkv[0], 'dp', axis=0, tiled=True)  96.1 us
    reduce_scatter x1, waiting for transfers between devices, body(): lax.psum_scatter(out_local, 'dp', scatter_dimension=1, tiled=True)  85.2 us
    ppermute x2, waiting for transfers between devices, shifted(): lax.ppermute(value, axis, [(source, source + steps) for source in range(i...  24.3 us
    unnamed x9, local copies, waits for them, and re-layouts  21.6 us
    dot_general x1, matrix products, section_work(): jnp.dot(flat_grads, weight_flat.T, preferred_element_type=jnp.float32)  12.2 us
    all_to_all x2, starting transfers between devices, sum_at_owner(): tiles = lax.all_to_all(in_blocks(value, dim, count), axis, 0, 0, tiled=True)  11.6 us
  transfers between devices with their start and end apart: 8, of which 8 were waited for; matrix products, arithmetic and copies ran while one was open for 2% of the time, Pallas kernels for 0%

commit v1 on v0

--- a/solution.py
+++ b/solution.py
@@ -101,7 +101,14 @@
         gate_term = mod_rows[1]
         d_branch = (gate_term * d_output.astype(jnp.float32)).astype(jnp.bfloat16)
         d_branch = jnp.where(is_live, d_branch, jnp.zeros_like(d_branch))
-        branch_full = lax.all_gather(d_branch, "seq", axis=0, tiled=True)
+        ring = [d_branch]
+        for hop in range(3):
+            ring.append(lax.ppermute(ring[-1], "seq", [(dev, (dev + 1) % 4) for dev in range(4)]))
+        branch_full = jnp.roll(
+            jnp.concatenate(ring[::-1], axis=0),
+            (lax.axis_index("seq") + 1) * ring[0].shape[0],
+            axis=0,
+        )
         live_length = lengths[slot_index]
         live_keys = key_positions < live_length
         saved_rows = lax.dynamic_index_in_dim(saved_all, slot_index, 0, False)

time: 576 us -> 659 us (1.14)
  blocking collectives: 0 us -> 156 us
  waiting for transfers between devices: 445 us -> 347 us
  other arithmetic: 33.7 us -> 50.4 us
  local copies, waits for them, and re-layouts: 37.6 us -> 52 us
  starting transfers between devices: 14.5 us -> 5.08 us
    all_to_all x0 -> x2, blocking collectives: none -> 156 us  [sum_at_owner(): tiles = lax.all_to_all(in_blocks(value, dim, count), axis, 0, 0, tiled=True)]
    ppermute x0 -> x6, waiting for transfers between devices: none -> 148 us  [section_work(): lax.ppermute(ring[-1], 'seq', [(dev, (dev + 1) % 4) for dev in range(4)])]
    all_to_all x2 -> x0, waiting for transfers between devices: 140 us -> none  [sum_at_owner(): tiles = lax.all_to_all(in_blocks(value, dim, count), axis, 0, 0, tiled=True)]
    all_gather x2 -> x0, waiting for transfers between devices: 99 us -> none  [section_work(): branch_full = lax.all_gather(d_branch, 'seq', axis=0, tiled=True)]
    broadcast_in_dim x6, other arithmetic: 7.43 us -> 26.3 us  [put_slot(): lax.dynamic_update_index_in_dim(store, jnp.where(is_live, fresh, older),...]
    while x36 -> x46, local copies, waits for them, and re-layouts: 2.82 us -> 17.2 us
    all_to_all x2 -> x0, starting transfers between devices: 11.6 us -> none  [sum_at_owner(): tiles = lax.all_to_all(in_blocks(value, dim, count), axis, 0, 0, tiled=True)]
  transfers between devices with their start and end apart: 8 -> 10, of which waited for: 8 -> 10; matrix products, arithmetic and copies ran while one was open for 2% -> 2% of each run, Pallas kernels for 0% -> 0%
where the time goes in v1:
time: 659 us; the launch traced here: 657 us
  waiting for transfers between devices  347 us (53%)
  blocking collectives  156 us (24%)
  local copies, waits for them, and re-layouts  52 us (8%)
  other arithmetic  50.4 us (8%)
  matrix products  30.6 us (5%)
  between operations  14.7 us (2%)
    all_to_all x2, blocking collectives, sum_at_owner(): tiles = lax.all_to_all(in_blocks(value, dim, count), axis, 0, 0, tiled=True)  156 us
    ppermute x6, waiting for transfers between devices, section_work(): lax.ppermute(ring[-1], 'seq', [(dev, (dev + 1) % 4) for dev in range(4)])  148 us
    all_gather x1, waiting for transfers between devices, body(): weight_rows = lax.all_gather(w_qkv[0], 'dp', axis=0, tiled=True)  96 us
    reduce_scatter x1, waiting for transfers between devices, body(): lax.psum_scatter(out_local, 'dp', scatter_dimension=1, tiled=True)  82.4 us
    broadcast_in_dim x6, other arithmetic, put_slot(): lax.dynamic_update_index_in_dim(store, jnp.where(is_live, fresh, older),...  26.3 us
    unnamed x9, local copies, waits for them, and re-layouts  21.7 us
    ppermute x2, waiting for transfers between devices, shifted(): lax.ppermute(value, axis, [(source, source + steps) for source in range(i...  20.8 us
    while x46, local copies, waits for them, and re-layouts  17.2 us
  transfers between devices with their start and end apart: 10, of which 10 were waited for; matrix products, arithmetic and copies ran while one was open for 2% of the time, Pallas kernels for 0%

profile of v1, /device:TPU:0, one launch (start us, length us, event | category | flops | bytes accessed | tf_op | source)
XLA Modules:
  0.0 657.1 jit_solution(9475358768180948924)
XLA Ops:
  7.2 2.4 copy.33
  10.4 2.6 copy.32
  13.7 3.3 fusion.29
  17.0 96.0 %all-gather.3.cloned.1.call-done = bf16[1,4096,3,512]{1,3,2,0:T(8,128)(2,1)} async-done(((bf16[1,256,3,512]{1,3,2,0:T(8,128)(2,1)}), bf16[1,4096,3,512]{1,3,2,0:T(8,128)(2,1)}) %all-gather.3.cloned.1.call-update) | async-done | bytes 12582928 | tf_op jit(solution)/shard_map/all_gather | solution.py:84
  113.0 16.6 %copy.34 = bf16[4096,1536]{1,0:T(8,128)(2,1)} copy(bf16[4096,1536]{0,1:T(8,128)(2,1)} %bitcast.151) | data formatting | bytes 25165824
  129.7 2.5 broadcast_in_dim.92
  134.1 424.0 %while.22 = (s32[]{:T(128)}, bf16[128,4096]{1,0:T(8,128)(2,1)S(1)}, bf16[1,128,4096]{2,1,0:T(8,128)(2,1)}, bf16[1,512,512]{1,2,0:T(8,128)(2,1)}, bf16[1,512,4096...) while((s32[]{:T(128)}, bf16[128,4096]{1,0:T(8,128)(2,1)S(1)}, ...), condition=%wide.region_12.13_spmd.clone, body=%wide.region_2.12_spmd.clone.sunk | while | flops 10230434816 | bytes 266504880 | solution.py:181
  134.5 1.5 collective-permute-start
  136.1 23.8 %collective-permute-done = bf16[128,4096]{1,0:T(8,128)(2,1)S(1)} collective-permute-done((bf16[128,4096]{1,0:T(8,128)(2,1)S(1)}, bf16[128,4096]{1,0:T(8,128)(2,1)S(1)}, u32[]{:S(2)}, u32[]{:S(2)}) %collective-permute-start) | collective-permute-done | bytes 1048608 | tf_op jit(solution)/shard_map/while/body/eval_jaxpr/ppermute | solution.py:106
  161.1 24.2 %collective-permute-done.1 = bf16[128,4096]{1,0:T(8,128)(2,1)} collective-permute-done((bf16[128,4096]{1,0:T(8,128)(2,1)S(1)}, bf16[128,4096]{1,0:T(8,128)(2,1)}, u32[]{:S(2)}, u32[]{:S(2)}) %collective-permute-start.1) | collective-permute-done | bytes 1048608 | tf_op jit(solution)/shard_map/while/body/eval_jaxpr/ppermute | solution.py:106
  185.2 23.7 %collective-permute-done.2 = bf16[128,4096]{1,0:T(8,128)(2,1)} collective-permute-done((bf16[128,4096]{1,0:T(8,128)(2,1)}, bf16[128,4096]{1,0:T(8,128)(2,1)}, u32[]{:S(2)}, u32[]{:S(2)}) %collective-permute-start.2) | collective-permute-done | bytes 1048608 | tf_op jit(solution)/shard_map/while/body/eval_jaxpr/ppermute | solution.py:106
  210.3 1.3 constant_dynamic-update-slice_fusion.17
  211.8 1.3 constant_dynamic-update-slice_fusion.20
  213.1 1.3 constant_dynamic-update-slice_fusion.21
  214.6 7.8 %fusion.61 = (bf16[1,512,4096]{2,1,0:T(8,128)(2,1)}, bf16[512,4096]{1,0:T(8,128)(2,1)}) fusion(bf16[1,512,4096]{2,1,0:T(8,128)(2,1)} %get-tuple-element.656, pred[]{:T(512)S(6)} %and.35, bf16[1024,4096]{1,0:T(8,128)(2,1)S(1)} %constant_dynamic-update-slice_fusion.23, s32[]{:T(128)S(6)} %select_n.250), kind=kLoop, calls=%fused_computation.27.clone.1 | loop fusion | flops 2097152 | bytes 16777220 | tf_op jit(solution)/shard_map/while/body/eval_jaxpr/jit(dynamic_update_index_in_dim)/broadcast_in_dim | solution.py:157
  222.4 1.3 conditional.6
  224.5 4.3 conditional.7
  224.5 4.3 broadcast.158
  228.8 82.3 %all_to_all.14 = f32[4,128,4096]{2,1,0:T(8,128)} all-to-all(f32[4,128,4096]{2,1,0:T(8,128)} %bitcast.137), channel_id=1, replica_groups=mesh['section'=2,'seq'=4,'dp'=16] {'seq'}, dimensions={0} | all-to-all | bytes 16777216 | tf_op jit(solution)/shard_map/while/body/eval_jaxpr/all_to_all | solution.py:18
  311.2 4.2 reduce_sum.88
  315.4 2.1 multiply_reduce_fusion.2
  317.8 3.4 fusion.62
  323.5 1.9 fusion.63
  325.4 19.4 %collective-permute-done.3 = bf16[128,4096]{1,0:T(8,128)(2,1)S(1)} collective-permute-done((bf16[128,4096]{1,0:T(8,128)(2,1)}, bf16[128,4096]{1,0:T(8,128)(2,1)S(1)}, u32[]{:S(2)}, u32[]{:S(2)}) %collective-permute-start.3) | collective-permute-done | bytes 1048608 | tf_op jit(solution)/shard_map/while/body/eval_jaxpr/ppermute | solution.py:25
  345.8 25.8 %collective-permute-done = bf16[128,4096]{1,0:T(8,128)(2,1)S(1)} collective-permute-done((bf16[128,4096]{1,0:T(8,128)(2,1)S(1)}, bf16[128,4096]{1,0:T(8,128)(2,1)S(1)}, u32[]{:S(2)}, u32[]{:S(2)}) %collective-permute-start) | collective-permute-done | bytes 1048608 | tf_op jit(solution)/shard_map/while/body/eval_jaxpr/ppermute | solution.py:106
  372.6 25.7 %collective-permute-done.1 = bf16[128,4096]{1,0:T(8,128)(2,1)} collective-permute-done((bf16[128,4096]{1,0:T(8,128)(2,1)S(1)}, bf16[128,4096]{1,0:T(8,128)(2,1)}, u32[]{:S(2)}, u32[]{:S(2)}) %collective-permute-start.1) | collective-permute-done | bytes 1048608 | tf_op jit(solution)/shard_map/while/body/eval_jaxpr/ppermute | solution.py:106
  398.3 25.0 %collective-permute-done.2 = bf16[128,4096]{1,0:T(8,128)(2,1)} collective-permute-done((bf16[128,4096]{1,0:T(8,128)(2,1)}, bf16[128,4096]{1,0:T(8,128)(2,1)}, u32[]{:S(2)}, u32[]{:S(2)}) %collective-permute-start.2) | collective-permute-done | bytes 1048608 | tf_op jit(solution)/shard_map/while/body/eval_jaxpr/ppermute | solution.py:106
  424.6 1.3 constant_dynamic-update-slice_fusion.17
  426.1 1.3 constant_dynamic-update-slice_fusion.20
  427.4 1.3 constant_dynamic-update-slice_fusion.21
  428.9 7.8 %fusion.61 = (bf16[1,512,4096]{2,1,0:T(8,128)(2,1)}, bf16[512,4096]{1,0:T(8,128)(2,1)}) fusion(bf16[1,512,4096]{2,1,0:T(8,128)(2,1)} %get-tuple-element.656, pred[]{:T(512)S(6)} %and.35, bf16[1024,4096]{1,0:T(8,128)(2,1)S(1)} %constant_dynamic-update-slice_fusion.23, s32[]{:T(128)S(6)} %select_n.250), kind=kLoop, calls=%fused_computation.27.clone.1 | loop fusion | flops 2097152 | bytes 16777220 | tf_op jit(solution)/shard_map/while/body/eval_jaxpr/jit(dynamic_update_index_in_dim)/broadcast_in_dim | solution.py:157
  436.7 18.5 %conditional.6 = (bf16[512,512]{0,1:T(8,128)(2,1)S(1)}, bf16[512,1536]{0,1:T(8,128)(2,1)}) conditional(s32[]{:T(128)} %convert_element_type.176, () %tuple.90, (s32[1]{0:T(128)}, s32[512]{0:T(512)S(1)}, bf16[1,512,3,512]{1,3,2,0:T(8,128)(2,1)S(1)}, bf16[512,4096]{1,0:T(8,128)(2,1)}, bf16[512,4096]{1,0:T(8,128)(2,1)}) %tuple.105), branch_computations={%region_3.3_spmd, %region_4.6_spmd} | conditional | flops 3773561856 | bytes 110144792 | solution.py:128
  438.5 4.7 fusion.36
  443.2 3.0 fusion.7
  446.8 1.5 copy-done.19
  448.3 2.4 fusion.11
  453.8 1.3 pad_maximum_fusion
  456.0 12.3 %conditional.7 = (f32[512,4096]{1,0:T(8,128)}) conditional(s32[]{:T(128)} %convert_element_type.176, () %tuple.89, (bf16[512,1536]{0,1:T(8,128)(2,1)}, bf16[4096,1536]{1,0:T(8,128)(2,1)}) %tuple.92), branch_computations={%region_7.7_spmd, %region_8.8_spmd} | conditional | flops 6442450944 | bytes 22544392 | solution.py:130
  456.0 12.3 %fusion.37 = f32[512,4096]{1,0:T(8,128)} fusion(bf16[512,1536]{0,1:T(8,128)(2,1)} %get-tuple-element.441, bf16[4096,1536]{1,0:T(8,128)(2,1)} %get-tuple-element.377), kind=kOutput, calls=%fused_computation.74 | convolution fusion | flops 6442450944 | bytes 22544384 | tf_op jit(solution)/shard_map/while/body/eval_jaxpr/cond/branch_1_fun/dot_general | solution.py:132
  468.2 74.1 %all_to_all.14 = f32[4,128,4096]{2,1,0:T(8,128)} all-to-all(f32[4,128,4096]{2,1,0:T(8,128)} %bitcast.137), channel_id=1, replica_groups=mesh['section'=2,'seq'=4,'dp'=16] {'seq'}, dimensions={0} | all-to-all | bytes 16777216 | tf_op jit(solution)/shard_map/while/body/eval_jaxpr/all_to_all | solution.py:18
  542.3 4.2 reduce_sum.88
  546.5 2.1 multiply_reduce_fusion.2
  549.0 3.4 fusion.62
  554.6 2.1 fusion.63
  556.7 1.4 collective-permute-done.3
  558.1 7.9 %fusion.26 = f32[512,4096]{1,0:T(8,128)} fusion(bf16[1,512,4096]{2,1,0:T(8,128)(2,1)} %get-tuple-element.404, bf16[1,512,512]{1,2,0:T(8,128)(2,1)} %get-tuple-element.403), kind=kOutput, calls=%fused_computation.57 | convolution fusion | flops 2147483648 | bytes 13107200 | tf_op jit(solution)/shard_map/dot_general | solution.py:33
  566.0 82.4 %reduce-scatter.2.cloned.1.call-done = f32[512,256]{1,0:T(8,128)} async-done(((f32[512,4096]{1,0:T(8,128)}), f32[512,256]{1,0:T(8,128)}) %reduce-scatter.2.cloned.1.call-update) | async-done | bytes 524304 | tf_op jit(solution)/shard_map/reduce_scatter | solution.py:189
  648.5 1.8 convert_bitcast_fusion.1
  (101 shorter events, 23.5 us)
Async XLA Ops:
  7.2 5.8 copy-start.16
  7.2 6.5 copy-start.17
  7.2 105.9 %all-gather.3.cloned.1.call-start = ((), (), s32[]{:S(2)}) async-start(), calls=%async_computation.3 | async-start | bytes 13369344 | tf_op jit(solution)/shard_map/all_gather | solution.py:84
  9.7 638.8 %reduce-scatter.2.cloned.1.call-start = ((), (), s32[]{:S(2)}) async-start(), calls=%async_computation.2 | async-start | bytes 8912896 | tf_op jit(solution)/shard_map/reduce_scatter | solution.py:189
  129.7 4.5 copy-start.18
  134.1 77.6 %copy-start.1 = (bf16[128,4096]{1,0:T(8,128)(2,1)}, bf16[128,4096]{1,0:T(8,128)(2,1)S(1)}, u32[]{:S(2)}) copy-start(bf16[128,4096]{1,0:T(8,128)(2,1)S(1)} %get-tuple-element.653) | copy-start | bytes 3145732 | tf_op jit(solution)/shard_map/while
  134.5 25.3 %collective-permute-start = (bf16[128,4096]{1,0:T(8,128)(2,1)S(1)}, bf16[128,4096]{1,0:T(8,128)(2,1)S(1)}, u32[]{:S(2)}, u32[]{:S(2)}) collective-permute-start(bf16[128,4096]{1,0:T(8,128)(2,1)S(1)} %fusion.60), channel_id=1, source_target_pairs={{0,16},{16,32},{32,48},{48,0},{1,17},{17,33},{33,49},{49,1},{2,18}... | collective-permute-start | bytes 3145736 | tf_op jit(solution)/shard_map/while/body/eval_jaxpr/ppermute | solution.py:106
  159.8 1.0 copy-start.3
  160.8 24.4 %collective-permute-start.1 = (bf16[128,4096]{1,0:T(8,128)(2,1)S(1)}, bf16[128,4096]{1,0:T(8,128)(2,1)}, u32[]{:S(2)}, u32[]{:S(2)}) collective-permute-start(bf16[128,4096]{1,0:T(8,128)(2,1)S(1)} %collective-permute-done), channel_id=1, source_target_pairs={{0,16},{16,32},{32,48},{48,0},{1,17},{17,33},{33,49},{49,1},{2,18}... | collective-permute-start | bytes 3145736 | tf_op jit(solution)/shard_map/while/body/eval_jaxpr/ppermute | solution.py:106
  185.2 23.7 %collective-permute-start.2 = (bf16[128,4096]{1,0:T(8,128)(2,1)}, bf16[128,4096]{1,0:T(8,128)(2,1)}, u32[]{:S(2)}, u32[]{:S(2)}) collective-permute-start(bf16[128,4096]{1,0:T(8,128)(2,1)} %collective-permute-done.1), channel_id=1, source_target_pairs={{0,16},{16,32},{32,48},{48,0},{1,17},{17,33},{33,49},{49,1},{2,18}... | collective-permute-start | bytes 3145736 | tf_op jit(solution)/shard_map/while/body/eval_jaxpr/ppermute | solution.py:106
  185.2 26.3 %copy-start.4 = (bf16[128,4096]{1,0:T(8,128)(2,1)S(1)}, bf16[128,4096]{1,0:T(8,128)(2,1)}, u32[]{:S(2)}) copy-start(bf16[128,4096]{1,0:T(8,128)(2,1)} %copy-done.3) | copy-start | bytes 3145732 | tf_op jit(solution)/shard_map/while
  214.6 7.8 %copy-start.6 = (bf16[1,512,3,512]{1,3,2,0:T(8,128)(2,1)S(1)}, bf16[1,512,3,512]{1,3,2,0:T(8,128)(2,1)}, u32[]{:S(2)}) copy-start(bf16[1,512,3,512]{1,3,2,0:T(8,128)(2,1)} %get-tuple-element.687) | copy-start | bytes 4718596 | tf_op jit(solution)/shard_map/while
  223.7 0.8 copy-start.9
  315.3 2.2 copy-start
  315.4 2.5 copy-start.14
  321.2 1.0 copy-start.15
  322.2 22.6 %collective-permute-start.3 = (bf16[128,4096]{1,0:T(8,128)(2,1)}, bf16[128,4096]{1,0:T(8,128)(2,1)S(1)}, u32[]{:S(2)}, u32[]{:S(2)}) collective-permute-start(bf16[128,4096]{1,0:T(8,128)(2,1)} %get-tuple-element.620), channel_id=1, source_target_pairs={{64,0},{65,1},{66,2},{67,3},{68,4},{69,5},{70,6},{71,7},{72,8},{73... | collective-permute-start | bytes 3145736 | tf_op jit(solution)/shard_map/while/body/eval_jaxpr/ppermute | solution.py:25
  344.7 81.2 %copy-start.1 = (bf16[128,4096]{1,0:T(8,128)(2,1)}, bf16[128,4096]{1,0:T(8,128)(2,1)S(1)}, u32[]{:S(2)}) copy-start(bf16[128,4096]{1,0:T(8,128)(2,1)S(1)} %get-tuple-element.653) | copy-start | bytes 3145732 | tf_op jit(solution)/shard_map/while
  345.2 26.5 %collective-permute-start = (bf16[128,4096]{1,0:T(8,128)(2,1)S(1)}, bf16[128,4096]{1,0:T(8,128)(2,1)S(1)}, u32[]{:S(2)}, u32[]{:S(2)}) collective-permute-start(bf16[128,4096]{1,0:T(8,128)(2,1)S(1)} %fusion.60), channel_id=1, source_target_pairs={{0,16},{16,32},{32,48},{48,0},{1,17},{17,33},{33,49},{49,1},{2,18}... | collective-permute-start | bytes 3145736 | tf_op jit(solution)/shard_map/while/body/eval_jaxpr/ppermute | solution.py:106
  371.6 1.0 copy-start.3
  372.6 25.7 %collective-permute-start.1 = (bf16[128,4096]{1,0:T(8,128)(2,1)S(1)}, bf16[128,4096]{1,0:T(8,128)(2,1)}, u32[]{:S(2)}, u32[]{:S(2)}) collective-permute-start(bf16[128,4096]{1,0:T(8,128)(2,1)S(1)} %collective-permute-done), channel_id=1, source_target_pairs={{0,16},{16,32},{32,48},{48,0},{1,17},{17,33},{33,49},{49,1},{2,18}... | collective-permute-start | bytes 3145736 | tf_op jit(solution)/shard_map/while/body/eval_jaxpr/ppermute | solution.py:106
  398.3 25.0 %collective-permute-start.2 = (bf16[128,4096]{1,0:T(8,128)(2,1)}, bf16[128,4096]{1,0:T(8,128)(2,1)}, u32[]{:S(2)}, u32[]{:S(2)}) collective-permute-start(bf16[128,4096]{1,0:T(8,128)(2,1)} %collective-permute-done.1), channel_id=1, source_target_pairs={{0,16},{16,32},{32,48},{48,0},{1,17},{17,33},{33,49},{49,1},{2,18}... | collective-permute-start | bytes 3145736 | tf_op jit(solution)/shard_map/while/body/eval_jaxpr/ppermute | solution.py:106
  398.3 27.6 %copy-start.4 = (bf16[128,4096]{1,0:T(8,128)(2,1)S(1)}, bf16[128,4096]{1,0:T(8,128)(2,1)}, u32[]{:S(2)}) copy-start(bf16[128,4096]{1,0:T(8,128)(2,1)} %copy-done.3) | copy-start | bytes 3145732 | tf_op jit(solution)/shard_map/while
  428.9 7.8 %copy-start.6 = (bf16[1,512,3,512]{1,3,2,0:T(8,128)(2,1)S(1)}, bf16[1,512,3,512]{1,3,2,0:T(8,128)(2,1)}, u32[]{:S(2)}) copy-start(bf16[1,512,3,512]{1,3,2,0:T(8,128)(2,1)} %get-tuple-element.687) | copy-start | bytes 4718596 | tf_op jit(solution)/shard_map/while
  437.8 8.3 %copy-start.10 = (bf16[512,1,512]{0,2,1:T(8,128)(2,1)}, bf16[512,1,512]{0,2,1:T(8,128)(2,1)S(1)}, u32[]{:S(2)}) copy-start(bf16[512,1,512]{0,2,1:T(8,128)(2,1)S(1)} %get-tuple-element.496) | copy-start | bytes 1572868 | tf_op jit(solution)/shard_map/while/body/eval_jaxpr/cond
  443.2 3.0 copy-start.13
  443.2 3.6 copy-start.5
  443.2 5.1 copy-start.19
  446.6 4.0 copy-start.7
  448.3 2.4 copy-start.2
  450.7 1.0 copy-start.12
  450.7 1.5 copy-start.11
  452.2 3.0 copy-start.8
  455.1 0.8 copy-start.9
  546.5 2.2 copy-start
  546.5 2.5 copy-start.14
  552.4 1.0 copy-start.15
  553.3 4.8 collective-permute-start.3
Sparse Core Ops, SparseCore 0:
  10.7 102.2 all-gather.2
  566.2 82.2 reduce-scatter.1
